TPU v7x, 32 devices: a whole 2x2x4 slice. The times are simulated.
32 devices in a mesh: box: 8 (over z, y), nbr: 4 (over x, core).
Axes of the slice: x: 2, y: 2, z: 4, core: 2. Of those that a mesh axis runs over, the one named last changes fastest.
Arguments:
- self_block: float32 [64, 256, 256], P('box', 'nbr'), as said below
- ordering: int32 [64, 256], P('box'), may hold values from 0 to 255, each once within a row
- interp: float32 [64, 64, 192], P('box'), may hold values from -0.12 to 0.12
- near_band: float32 [64, 8, 2, 64, 256], P('box', 'nbr'), may hold values from -3 to 3
- pair_mask: int32 [64, 8], P('box', 'nbr'), may hold values 0 or 1
Outputs:
- skeleton_self: float32 [64, 64, 64], P('box')
- red_inverse: float32 [64, 192, 192], P('box', 'nbr')
- couplings: float32 [64, 8, 64, 128], P('box', 'nbr')
Inputs may be any that keep to these rules, and one draw needn't show every extreme that they name: Each row of ordering is a permutation of the 256 unknowns of its box. Each self_block[b] has a positive diagonal.
All inputs are finite; a program needn't handle non-finite values. No bound on the sum of `pair_mask` on one device may be relied on, other than what follows from the above.
Results may differ from a plain program's by a relative error of at most 0.0003.
Values sent between devices are 32-bit elements; how exact they have to be, the bound alone decides.
A program may use at most 128 MiB of HBM per device.

v0:
```python
import jax
import jax.numpy as jnp
from jax import lax
from jax.sharding import PartitionSpec as P

SKEL = 64
RED = 192
REACH = 4
NS_ITERS = 3


def extended_2(block, sides, width):
    for axis, dim in sides:
        count = lax.axis_size(axis)
        forward = [(i, i + 1) for i in range(count - 1)]
        forward.append((count - 1, 0))
        backward = [(target, source) for source, target in forward]
        low = lax.ppermute(
            lax.slice_in_dim(block, block.shape[dim] - width, None, axis=dim), axis, forward
        )
        high = lax.ppermute(lax.slice_in_dim(block, 0, width, axis=dim), axis, backward)
        block = jnp.concatenate([low, block, high], axis=dim)
    return block


def passed_along(block, axis, distance):
    devices = range(lax.axis_size(axis))
    route = [((i - distance) % len(devices), i) for i in devices]
    return lax.ppermute(block, axis, route)


def product(pattern, left_term, right_term):
    return jnp.einsum(pattern, left_term, right_term, precision=lax.Precision.HIGHEST)


def selector(ordering):
    columns = jnp.arange(ordering.shape[1], dtype=jnp.int32)
    return (ordering[:, :, None] == columns[None, None, :]).astype(jnp.float32)


def permuted(matrix, chooser):
    row_sorted = product("bik,bkj->bij", chooser, matrix)
    return product("bik,bjk->bij", row_sorted, chooser)


def factors(matrix, chooser, interp):
    full_block = permuted(matrix, chooser)
    skel_skel = full_block[:, :SKEL, :SKEL]
    skel_red = full_block[:, :SKEL, SKEL:]
    red_skel = full_block[:, SKEL:, :SKEL]
    red_red = full_block[:, SKEL:, SKEL:]
    skel_interp = product("bij,bjk->bik", skel_skel, interp)
    x_skel_red = skel_red - skel_interp
    x_red_skel = red_skel - product("bji,bjk->bik", interp, skel_skel)
    x_red_red = (
        red_red
        - product("bji,bjk->bik", interp, skel_red)
        - product("bij,bjk->bik", red_skel, interp)
    )
    x_red_red = x_red_red + product("bji,bjk->bik", interp, skel_interp)
    identity = jnp.eye(RED, dtype=jnp.float32)
    diag_vals = jnp.diagonal(red_red, axis1=1, axis2=2)
    approx = identity[None] / diag_vals[:, None, :]
    for sweep_index in range(NS_ITERS):
        approx = 2.0 * approx - product(
            "bij,bjk->bik", approx, product("bij,bjk->bik", x_red_red, approx)
        )
    left_factor = product("bij,bjk->bik", x_skel_red, approx)
    right_factor = product("bij,bjk->bik", approx, x_red_skel)
    own_block = skel_skel - product("bij,bjk->bik", left_factor, x_red_skel)
    return (approx, left_factor, right_factor, own_block)


def slot_terms(near_piece, chooser, interp, approx, left_factor, right_factor):
    both_parts = product("bpik,bjk->bpij", near_piece, chooser)
    row_part = both_parts[:, 0]
    col_part = both_parts[:, 1]
    near_red = row_part[:, :, SKEL:] - product("bij,bjk->bik", row_part[:, :, :SKEL], interp)
    red_near_t = col_part[:, :, SKEL:] - product("bij,bjk->bik", col_part[:, :, :SKEL], interp)
    new_forward = jnp.swapaxes(col_part[:, :, :SKEL], 1, 2) - product(
        "bij,bkj->bik", left_factor, red_near_t
    )
    new_backward = jnp.swapaxes(row_part[:, :, :SKEL], 1, 2) - product(
        "bji,bkj->bik", right_factor, near_red
    )
    coupled = jnp.concatenate([new_forward, new_backward], axis=2)
    update = product("bij,bkj->bik", product("bij,bjk->bik", near_red, approx), red_near_t)
    return (coupled, update)


def body(self_block, ordering, interp, near_band, pair_mask):
    box_count = ordering.shape[0]
    nbr_count = lax.axis_size("nbr")
    nbr_place = lax.axis_index("nbr")
    chooser = selector(ordering)
    share_boxes = box_count // nbr_count
    own_rows = lax.all_to_all(self_block, "nbr", split_axis=0, concat_axis=1, tiled=True)
    my_chooser = lax.dynamic_slice_in_dim(chooser, nbr_place * share_boxes, share_boxes, 0)
    my_interp = lax.dynamic_slice_in_dim(interp, nbr_place * share_boxes, share_boxes, 0)
    part_inverse, part_left, part_right, part_own = factors(own_rows, my_chooser, my_interp)
    approx, left_factor, right_factor, own_block = (
        lax.all_gather(part_inverse, "nbr", axis=0, tiled=True),
        lax.all_gather(part_left, "nbr", axis=0, tiled=True),
        lax.all_gather(part_right, "nbr", axis=0, tiled=True),
        lax.all_gather(part_own, "nbr", axis=0, tiled=True),
    )
    masked = near_band * pair_mask.astype(jnp.float32)[:, :, None, None, None]
    local_slots = near_band.shape[1]
    windows = []
    widened = extended_2(masked, (("box", 0),), REACH)
    for slot_index in range(local_slots):
        windows.append((widened[:, slot_index], REACH))
    extended = jnp.zeros((box_count + 2 * REACH, SKEL, SKEL), jnp.float32)
    couples = []
    for slot_index in range(local_slots):
        window, margin = windows[slot_index]
        global_slot = nbr_place * local_slots + slot_index
        offset = jnp.where(global_slot < REACH, global_slot - REACH, global_slot - REACH + 1)
        near_piece = lax.dynamic_slice_in_dim(window, margin - offset, box_count, 0)
        coupled, update = slot_terms(near_piece, chooser, interp, approx, left_factor, right_factor)
        couples.append(coupled)
        extended = extended + lax.dynamic_update_slice_in_dim(
            jnp.zeros_like(extended), update, REACH - offset, 0
        )
    incoming_right = passed_along(extended[:REACH], "box", -1)
    incoming_left = passed_along(extended[REACH + box_count :], "box", 1)
    owned_sum = extended[REACH : REACH + box_count]
    owned_sum = owned_sum.at[box_count - REACH :].add(incoming_right)
    owned_sum = owned_sum.at[:REACH].add(incoming_left)
    update_total = lax.psum(owned_sum, "nbr")
    skeleton_self = own_block - update_total
    row_count = approx.shape[1] // nbr_count
    red_inverse = lax.dynamic_slice_in_dim(approx, nbr_place * row_count, row_count, 1)
    return (skeleton_self, red_inverse, jnp.stack(couples, 1))


def solution(mesh):
    placed = (
        P("box", "nbr", None),
        P("box", None),
        P("box", None, None),
        P("box", "nbr", None, None, None),
        P("box", "nbr"),
    )
    return jax.shard_map(
        body,
        mesh=mesh,
        in_specs=placed,
        out_specs=(P("box", None, None), P("box", "nbr", None), P("box", "nbr", None, None)),
        check_vma=False,
    )
```

profile of v0, /device:TPU:0, one launch (start us, length us, event | category | flops | bytes accessed | tf_op | source)
XLA Modules:
  0.0 154.4 jit_solution(4811347467437603980)
XLA Ops:
  7.2 4.4 %all-to-all-start = ((f32[8,64,256]{2,1,0:T(8,128)}), f32[8,64,256]{2,1,0:T(8,128)S(1)}, u32[]{:S(2)}, u32[]{:S(2)}) async-start(f32[8,64,256]{2,1,0:T(8,128)} %param.9), calls=%async_computation | async-start | bytes 1048576 | tf_op jit(solution)/shard_map/all_to_all | solution.py:97
  12.3 1.9 %broadcast_multiply_fusion = f32[8,2,2,64,256]{4,3,2,1,0:T(8,128)S(1)} fusion(f32[8,2,2,64,256]{4,3,2,1,0:T(8,128)} %param.12, f32[8,2]{1,0:T(8,128)S(1)} %copy.79), kind=kLoop, calls=%fused_computation.31 | loop fusion | flops 524288 | bytes 4194368 | tf_op jit(solution)/shard_map/mul | solution.py:107
  14.2 1.5 fusion.50
  15.8 2.3 %collective-permute-start = (f32[4,2,2,64,256]{4,3,2,1,0:T(8,128)}, f32[4,2,2,64,256]{4,3,2,1,0:T(8,128)}, u32[]{:S(2)}, u32[]{:S(2)}) collective-permute-start(f32[4,2,2,64,256]{4,3,2,1,0:T(8,128)} %get-tuple-element.44), channel_id=1, source_target_pairs={{0,4},{4,8},{8,12},{12,16},{16,20},{20,24},{24,28},{28,0},{1,5},{5... | collective-permute-start | bytes 3145736 | tf_op jit(solution)/shard_map/ppermute | solution.py:18
  18.1 3.0 %collective-permute-start.1 = (f32[4,2,2,64,256]{4,3,2,1,0:T(8,128)}, f32[4,2,2,64,256]{4,3,2,1,0:T(8,128)}, u32[]{:S(2)}, u32[]{:S(2)}) collective-permute-start(f32[4,2,2,64,256]{4,3,2,1,0:T(8,128)} %get-tuple-element.45), channel_id=1, source_target_pairs={{4,0},{8,4},{12,8},{16,12},{20,16},{24,20},{28,24},{0,28},{5,1},{9... | collective-permute-start | bytes 3145736 | tf_op jit(solution)/shard_map/ppermute | solution.py:21
  23.0 1.4 fusion.12
  29.3 10.5 %copy.75 = f32[2,192,192]{0,2,1:T(8,128)} copy(f32[2,192,192]{2,1,0:T(8,128)} %slice.151) | data formatting | bytes 589824 | tf_op jit(solution)/shard_map/slice | solution.py:51
  39.8 5.2 %gather_fusion = f32[192,2]{1,0:T(8,128)} fusion(f32[2,192,192]{0,2,1:T(8,128)} %copy.75, s32[192]{0:T(256)S(1)} %bitcast.80), kind=kCustom, calls=%fused_computation | custom fusion | bytes 4608 | tf_op jit(solution)/shard_map/jit(diagonal)/gather | solution.py:62
  46.0 1.5 convolution_add_fusion
  47.5 1.5 fusion.14
  51.7 2.1 %fusion.28 = f32[2,64,192]{2,1,0:T(8,128)} fusion(f32[2,192,192]{2,1,0:T(8,128)S(1)} %convolution_subtract_fusion.6, f32[2,64,192]{2,1,0:T(8,128)} %fusion.36, f32[2,256,256]{2,1,0:T(8,128)S(1)} %fusion.10), kind=kOutput, calls=%fused_computation.61 | convolution fusion | flops 56647680 | bytes 720896 | tf_op jit(solution)/shard_map/bij,bjk->bik/dot_general | solution.py:33
  53.9 1.8 %copy.96 = f32[2,192,64]{1,2,0:T(8,128)} copy(f32[2,192,64]{2,1,0:T(8,128)} %slice.152) | data formatting | bytes 196608
  58.0 7.4 %all_gather.12 = f32[8,64,64]{2,1,0:T(8,128)} all-gather(f32[2,64,64]{2,1,0:T(8,128)S(1)} %convolution_subtract_fusion.14), channel_id=1, replica_groups=mesh['box'=8,'nbr'=4] {'nbr'}, dimensions={0}, use_global_device_ids=true | all-gather | bytes 163840 | tf_op jit(solution)/shard_map/all_gather | solution.py:105
  65.4 10.1 %all_gather.14 = f32[8,64,192]{2,1,0:T(8,128)S(1)} all-gather(f32[2,64,192]{2,1,0:T(8,128)} %fusion.28), channel_id=1, replica_groups=mesh['box'=8,'nbr'=4] {'nbr'}, dimensions={0}, use_global_device_ids=true | all-gather | bytes 491520 | tf_op jit(solution)/shard_map/all_gather | solution.py:103
  76.0 7.5 %all_gather.15 = f32[8,192,64]{1,2,0:T(8,128)S(1)} all-gather(f32[2,192,64]{1,2,0:T(8,128)S(1)} %fusion.56), channel_id=1, replica_groups=mesh['box'=8,'nbr'=4] {'nbr'}, dimensions={0}, use_global_device_ids=true | all-gather | bytes 491520 | tf_op jit(solution)/shard_map/all_gather | solution.py:104
  83.5 2.0 %pad_maximum_fusion = f32[16,2,2,64,256]{4,3,2,1,0:T(8,128)S(1)} fusion(f32[4,2,2,64,256]{4,3,2,1,0:T(8,128)} %collective-permute-done.1, f32[8,2,2,64,256]{4,3,2,1,0:T(8,128)S(1)} %broadcast_multiply_fusion, f32[4,2,2,64,256]{4,3,2,1,0:T(8,128)} %collective-permute-done), kind=kLoop, calls=%fused_computation.1 | loop fusion | flops 2097152 | bytes 8388608 | tf_op jit(solution)/shard_map/concatenate | solution.py:22
  85.9 1.6 %fusion.2 = f32[8,2,64,256]{3,2,0,1:T(8,128)S(1)} fusion(s32[8,256]{1,0:T(8,128)S(1)} %copy-done.14, f32[16,1,2,64,256]{4,3,2,1,0:T(8,128)S(1)} %get-tuple-element.42, s32[]{:T(128)S(6)} %select_n.30), kind=kOutput, calls=%fused_computation.5 | convolution fusion | flops 805830656 | bytes 2105348 | tf_op jit(solution)/shard_map/bpik,bjk->bpij/dot_general | solution.py:33
  88.2 1.6 %fusion = f32[8,2,64,256]{3,2,1,0:T(8,128)S(1)} fusion(f32[16,1,2,64,256]{4,3,2,1,0:T(8,128)S(1)} %get-tuple-element.43, s32[]{:T(128)S(6)} %select_n.28, s32[8,256]{1,0:T(8,128)S(1)} %copy-done.14), kind=kOutput, calls=%fused_computation.3 | convolution fusion | flops 805830656 | bytes 2105348 | tf_op jit(solution)/shard_map/bpik,bjk->bpij/dot_general | solution.py:33
  95.5 2.8 %fusion.54 = f32[8,64,192]{2,1,0:T(8,128)S(1)} fusion(f32[8,64,192]{2,1,0:T(8,128)} %copy-done.4, f32[8,192,192]{2,1,0:T(8,128)} %all-gather.2.cloned.1.call-done), kind=kOutput, calls=%fused_computation.89 | convolution fusion | flops 226492416 | bytes 1966080 | tf_op jit(solution)/shard_map/bij,bjk->bik/dot_general | solution.py:33
  101.7 2.3 %collective-permute-start.2 = (f32[4,64,64]{2,1,0:T(8,128)S(1)}, f32[4,64,64]{2,1,0:T(8,128)S(1)}, u32[]{:S(2)}, u32[]{:S(2)}) collective-permute-start(f32[4,64,64]{2,1,0:T(8,128)S(1)} %get-tuple-element.51), channel_id=1, source_target_pairs={{4,0},{8,4},{12,8},{16,12},{20,16},{24,20},{28,24},{0,28},{5,1},{9... | collective-permute-start | bytes 196616 | tf_op jit(solution)/shard_map/ppermute | solution.py:29
  105.0 2.4 %copy.87 = f32[8,2,64,128]{3,2,1,0:T(8,128)} copy(f32[8,2,64,128]{2,3,0,1:T(8,128)} %pad_maximum_fusion.1) | data formatting | bytes 1048576
  107.5 8.1 %collective-permute-done.3 = f32[4,64,64]{2,1,0:T(8,128)S(1)} collective-permute-done((f32[4,64,64]{2,1,0:T(8,128)S(1)}, f32[4,64,64]{2,1,0:T(8,128)S(1)}, u32[]{:S(2)}, u32[]{:S(2)}) %collective-permute-start.3) | collective-permute-done | bytes 65568 | tf_op jit(solution)/shard_map/ppermute | solution.py:29
  117.2 28.7 %all-reduce.2.cloned.1.call-done = f32[8,64,64]{2,1,0:T(8,128)} async-done(((f32[8,64,64]{2,1,0:T(8,128)}), f32[8,64,64]{2,1,0:T(8,128)}) %all-reduce.2.cloned.1.call-update) | async-done | bytes 131088 | tf_op jit(solution)/shard_map/psum | solution.py:130
  145.9 1.7 %sub.80 = f32[8,64,64]{2,1,0:T(8,128)} subtract(f32[8,64,64]{2,1,0:T(8,128)S(1)} %copy-done.12, f32[8,64,64]{2,1,0:T(8,128)} %all-reduce.2.cloned.1.call-done) | non-fusion elementwise | flops 32768 | bytes 393216 | tf_op jit(solution)/shard_map/sub | solution.py:131
  (83 shorter events, 26.9 us)
Async XLA Ops:
  7.2 18.5 %copy-start = (f32[8,64,192]{2,1,0:T(8,128)S(1)}, f32[8,64,192]{2,1,0:T(8,128)}, u32[]{:S(2)}) copy-start(f32[8,64,192]{2,1,0:T(8,128)} %param.11) | copy-start | bytes 1179652
  7.2 15.8 %all-to-all-start = ((f32[8,64,256]{2,1,0:T(8,128)}), f32[8,64,256]{2,1,0:T(8,128)S(1)}, u32[]{:S(2)}, u32[]{:S(2)}) async-start(f32[8,64,256]{2,1,0:T(8,128)} %param.9), calls=%async_computation | async-start | bytes 1048576 | tf_op jit(solution)/shard_map/all_to_all | solution.py:97
  11.6 83.9 %all-gather.2.cloned.1.call-start = ((), (), s32[]{:S(2)}) async-start(), calls=%async_computation.1 | async-start | bytes 1966080 | tf_op jit(solution)/shard_map/all_gather | solution.py:102
  14.2 7.6 %copy-start.14 = (s32[8,256]{1,0:T(8,128)S(1)}, s32[8,256]{1,0:T(8,128)}, u32[]{:S(2)}) copy-start(s32[8,256]{1,0:T(8,128)} %param.10) | copy-start | bytes 24580
  15.8 67.7 %collective-permute-start = (f32[4,2,2,64,256]{4,3,2,1,0:T(8,128)}, f32[4,2,2,64,256]{4,3,2,1,0:T(8,128)}, u32[]{:S(2)}, u32[]{:S(2)}) collective-permute-start(f32[4,2,2,64,256]{4,3,2,1,0:T(8,128)} %get-tuple-element.44), channel_id=1, source_target_pairs={{0,4},{4,8},{8,12},{12,16},{16,20},{20,24},{24,28},{28,0},{1,5},{5... | collective-permute-start | bytes 3145736 | tf_op jit(solution)/shard_map/ppermute | solution.py:18
  18.1 65.4 %collective-permute-start.1 = (f32[4,2,2,64,256]{4,3,2,1,0:T(8,128)}, f32[4,2,2,64,256]{4,3,2,1,0:T(8,128)}, u32[]{:S(2)}, u32[]{:S(2)}) collective-permute-start(f32[4,2,2,64,256]{4,3,2,1,0:T(8,128)} %get-tuple-element.45), channel_id=1, source_target_pairs={{4,0},{8,4},{12,8},{16,12},{20,16},{24,20},{28,24},{0,28},{5,1},{9... | collective-permute-start | bytes 3145736 | tf_op jit(solution)/shard_map/ppermute | solution.py:21
  46.0 3.0 %copy-start.13 = (f32[192,192]{1,0:T(8,128)S(1)}, f32[192,192]{1,0:T(8,128)}, u32[]{:S(2)}) copy-start(f32[192,192]{1,0:T(8,128)} %fusion.25) | copy-start | bytes 442372
  51.7 2.1 %copy-start.2 = (f32[2,192,192]{2,1,0:T(8,128)}, f32[2,192,192]{2,1,0:T(8,128)S(1)}, u32[]{:S(2)}) copy-start(f32[2,192,192]{2,1,0:T(8,128)S(1)} %convolution_subtract_fusion.6) | copy-start | bytes 884740
  53.8 21.7 %copy-start.3 = (f32[2,192,192]{2,1,0:T(8,128)S(1)}, f32[2,192,192]{2,1,0:T(8,128)}, u32[]{:S(2)}) copy-start(f32[2,192,192]{2,1,0:T(8,128)} %copy-done.2) | copy-start | bytes 884740
  53.8 92.0 %all-reduce.2.cloned.1.call-start = ((), (), s32[]{:S(2)}) async-start(), calls=%async_computation.2 | async-start | bytes 524288 | tf_op jit(solution)/shard_map/psum | solution.py:130
  88.2 3.5 %copy-start.5 = (f32[8,64,192]{2,1,0:T(8,128)}, f32[8,64,192]{2,1,0:T(8,128)S(1)}, u32[]{:S(2)}) copy-start(f32[8,64,192]{2,1,0:T(8,128)S(1)} %convolution_subtract_fusion) | copy-start | bytes 1179652
  91.7 2.0 %copy-start.4 = (f32[8,64,192]{2,1,0:T(8,128)}, f32[8,64,192]{2,1,0:T(8,128)S(1)}, u32[]{:S(2)}) copy-start(f32[8,64,192]{2,1,0:T(8,128)S(1)} %convolution_subtract_fusion.3) | copy-start | bytes 1179652
  95.5 3.5 %copy-start.1 = (f32[8,192,192]{2,1,0:T(8,128)S(1)}, f32[8,192,192]{2,1,0:T(8,128)}, u32[]{:S(2)}) copy-start(f32[8,192,192]{2,1,0:T(8,128)} %all-gather.2.cloned.1.call-done) | copy-start | bytes 3538948
  98.3 1.8 %copy-start.6 = (f32[8,64,192]{2,1,0:T(8,128)S(1)}, f32[8,64,192]{2,1,0:T(8,128)}, u32[]{:S(2)}) copy-start(f32[8,64,192]{2,1,0:T(8,128)} %copy-done.5) | copy-start | bytes 1179652
  99.0 4.9 %copy-start.9 = (f32[8,1,64,128]{2,3,0,1:T(8,128)S(1)}, f32[8,1,64,128]{2,3,0,1:T(8,128)}, u32[]{:S(2)}) copy-start(f32[8,1,64,128]{2,3,0,1:T(8,128)} %get-tuple-element.52) | copy-start | bytes 786436
  99.0 4.9 %copy-start.10 = (f32[8,1,64,128]{2,3,0,1:T(8,128)S(1)}, f32[8,1,64,128]{2,3,0,1:T(8,128)}, u32[]{:S(2)}) copy-start(f32[8,1,64,128]{2,3,0,1:T(8,128)} %get-tuple-element.53) | copy-start | bytes 786436
  100.8 0.8 copy-start.7
  101.7 5.7 %copy-start.8 = (f32[16,64,64]{2,1,0:T(8,128)S(1)}, f32[16,64,64]{2,1,0:T(8,128)}, u32[]{:S(2)}) copy-start(f32[16,64,64]{2,1,0:T(8,128)} %copy-done.7) | copy-start | bytes 786436
  101.7 5.8 %collective-permute-start.2 = (f32[4,64,64]{2,1,0:T(8,128)S(1)}, f32[4,64,64]{2,1,0:T(8,128)S(1)}, u32[]{:S(2)}, u32[]{:S(2)}) collective-permute-start(f32[4,64,64]{2,1,0:T(8,128)S(1)} %get-tuple-element.51), channel_id=1, source_target_pairs={{4,0},{8,4},{12,8},{16,12},{20,16},{24,20},{28,24},{0,28},{5,1},{9... | collective-permute-start | bytes 196616 | tf_op jit(solution)/shard_map/ppermute | solution.py:29
  105.0 40.9 %copy-start.12 = (f32[8,64,64]{2,1,0:T(8,128)S(1)}, f32[8,64,64]{2,1,0:T(8,128)}, u32[]{:S(2)}) copy-start(f32[8,64,64]{2,1,0:T(8,128)} %all_gather.12) | copy-start | bytes 393220
  107.4 8.2 %collective-permute-start.3 = (f32[4,64,64]{2,1,0:T(8,128)S(1)}, f32[4,64,64]{2,1,0:T(8,128)S(1)}, u32[]{:S(2)}, u32[]{:S(2)}) collective-permute-start(f32[4,64,64]{2,1,0:T(8,128)S(1)} %get-tuple-element.50), channel_id=1, source_target_pairs={{28,0},{0,4},{4,8},{8,12},{12,16},{16,20},{20,24},{24,28},{29,1},{... | collective-permute-start | bytes 196616 | tf_op jit(solution)/shard_map/ppermute | solution.py:29
  115.7 0.7 copy-start.11
Sparse Core Ops, SparseCore 0:
  53.9 20.9 all-gather.1
  116.5 29.3 all-reduce.1
where the time goes:
time: 155 us; the launch traced here: 154 us
  waiting for transfers between devices  36.9 us (24%)
  matrix products  28.6 us (18%)
  local copies, waits for them, and re-layouts  27.1 us (17%)
  blocking collectives  24.9 us (16%)
  between operations  14.5 us (9%)
  starting transfers between devices  12.1 us (8%)
  other arithmetic  10.3 us (7%)
    psum x1, waiting for transfers between devices, body(): update_total = lax.psum(owned_sum, 'nbr')  28.7 us
    dot_general x30, matrix products, product(): jnp.einsum(pattern, left_term, right_term, precision=lax.Precision.HIGHEST)  28.6 us
    slice x2, local copies, waits for them, and re-layouts, factors(): red_red = full_block[:, SKEL:, SKEL:]  11.4 us
    all_gather x1, blocking collectives, body(): lax.all_gather(part_left, 'nbr', axis=0, tiled=True)  10.1 us
    ppermute x2, waiting for transfers between devices, passed_along(): return lax.ppermute(block, axis, route)  8.12 us
    all_gather x1, blocking collectives, body(): lax.all_gather(part_right, 'nbr', axis=0, tiled=True)  7.46 us
    all_gather x1, blocking collectives, body(): lax.all_gather(part_own, 'nbr', axis=0, tiled=True)  7.4 us
    unnamed x33, local copies, waits for them, and re-layouts  6.4 us
  transfers between devices with their start and end apart: 7, of which 2 were waited for; matrix products, arithmetic and copies ran while one was open for 37% of the time, Pallas kernels for 0%

commit v1 on v0

--- a/solution.py
+++ b/solution.py
@@ -127,7 +127,11 @@
     owned_sum = extended[REACH : REACH + box_count]
     owned_sum = owned_sum.at[box_count - REACH :].add(incoming_right)
     owned_sum = owned_sum.at[:REACH].add(incoming_left)
-    update_total = lax.psum(owned_sum, "nbr")
+    update_total = owned_sum
+    for hop in (1, 2):
+        update_total = update_total + lax.ppermute(
+            update_total, "nbr", [(dev, dev ^ hop) for dev in range(4)]
+        )
     skeleton_self = own_block - update_total
     row_count = approx.shape[1] // nbr_count
     red_inverse = lax.dynamic_slice_in_dim(approx, nbr_place * row_count, row_count, 1)

time: 155 us -> 130 us (0.84)
  waiting for transfers between devices: 36.9 us -> 12.4 us
  other arithmetic: 10.3 us -> 8.41 us
    psum x1 -> x0, waiting for transfers between devices: 28.7 us -> none  [body(): update_total = lax.psum(owned_sum, 'nbr')]
    ppermute x0 -> x2, waiting for transfers between devices: none -> 4.26 us  [body(): lax.ppermute(update_total, 'nbr', [(dev, dev ^ hop) for dev in range(4)])]
    unnamed x33 -> x37, local copies, waits for them, and re-layouts: 6.4 us -> 4.87 us
  transfers between devices with their start and end apart: 7 -> 8, of which waited for: 2 -> 4; matrix products, arithmetic and copies ran while one was open for 37% -> 45% of each run, Pallas kernels for 0% -> 0%
where the time goes in v1:
time: 130 us; the launch traced here: 129 us
  matrix products  29.9 us (23%)
  local copies, waits for them, and re-layouts  25.6 us (20%)
  blocking collectives  24.9 us (19%)
  between operations  14.5 us (11%)
  starting transfers between devices  13.4 us (10%)
  waiting for transfers between devices  12.4 us (10%)
  other arithmetic  8.41 us (6%)
    dot_general x30, matrix products, product(): jnp.einsum(pattern, left_term, right_term, precision=lax.Precision.HIGHEST)  29.9 us
    slice x2, local copies, waits for them, and re-layouts, factors(): red_red = full_block[:, SKEL:, SKEL:]  11.4 us
    all_gather x1, blocking collectives, body(): lax.all_gather(part_left, 'nbr', axis=0, tiled=True)  10.1 us
    ppermute x2, waiting for transfers between devices, passed_along(): return lax.ppermute(block, axis, route)  8.13 us
    all_gather x1, blocking collectives, body(): lax.all_gather(part_right, 'nbr', axis=0, tiled=True)  7.46 us
    all_gather x1, blocking collectives, body(): lax.all_gather(part_own, 'nbr', axis=0, tiled=True)  7.37 us
    gather x2, local copies, waits for them, and re-layouts, factors(): diag_vals = jnp.diagonal(red_red, axis1=1, axis2=2)  6.28 us
    unnamed x37, local copies, waits for them, and re-layouts  4.87 us
  transfers between devices with their start and end apart: 8, of which 4 were waited for; matrix products, arithmetic and copies ran while one was open for 45% of the time, Pallas kernels for 0%

profile of v1, /device:TPU:0, one launch (start us, length us, event | category | flops | bytes accessed | tf_op | source)
XLA Modules:
  0.0 129.2 jit_solution(12754254190852601218)
XLA Ops:
  7.2 4.4 %all-to-all-start = ((f32[8,64,256]{2,1,0:T(8,128)}), f32[8,64,256]{2,1,0:T(8,128)S(1)}, u32[]{:S(2)}, u32[]{:S(2)}) async-start(f32[8,64,256]{2,1,0:T(8,128)} %param.9), calls=%async_computation | async-start | bytes 1048576 | tf_op jit(solution)/shard_map/all_to_all | solution.py:97
  12.3 1.9 %broadcast_multiply_fusion = f32[8,2,2,64,256]{4,3,2,1,0:T(8,128)S(1)} fusion(f32[8,2,2,64,256]{4,3,2,1,0:T(8,128)} %param.12, f32[8,2]{1,0:T(8,128)S(1)} %copy.79), kind=kLoop, calls=%fused_computation.31 | loop fusion | flops 524288 | bytes 4194368 | tf_op jit(solution)/shard_map/mul | solution.py:107
  14.2 1.5 %fusion.50 = (f32[4,2,2,64,256]{4,3,2,1,0:T(8,128)}, f32[4,2,2,64,256]{4,3,2,1,0:T(8,128)}) fusion(f32[8,2,2,64,256]{4,3,2,1,0:T(8,128)S(1)} %broadcast_multiply_fusion), kind=kLoop, calls=%fused_computation.86 | loop fusion | bytes 4194304 | tf_op jit(solution)/shard_map/slice | solution.py:19
  15.8 2.3 %collective-permute-start = (f32[4,2,2,64,256]{4,3,2,1,0:T(8,128)}, f32[4,2,2,64,256]{4,3,2,1,0:T(8,128)}, u32[]{:S(2)}, u32[]{:S(2)}) collective-permute-start(f32[4,2,2,64,256]{4,3,2,1,0:T(8,128)} %get-tuple-element.44), channel_id=1, source_target_pairs={{0,4},{4,8},{8,12},{12,16},{16,20},{20,24},{24,28},{28,0},{1,5},{5... | collective-permute-start | bytes 3145736 | tf_op jit(solution)/shard_map/ppermute | solution.py:18
  18.1 3.0 %collective-permute-start.1 = (f32[4,2,2,64,256]{4,3,2,1,0:T(8,128)}, f32[4,2,2,64,256]{4,3,2,1,0:T(8,128)}, u32[]{:S(2)}, u32[]{:S(2)}) collective-permute-start(f32[4,2,2,64,256]{4,3,2,1,0:T(8,128)} %get-tuple-element.45), channel_id=1, source_target_pairs={{4,0},{8,4},{12,8},{16,12},{20,16},{24,20},{28,24},{0,28},{5,1},{9... | collective-permute-start | bytes 3145736 | tf_op jit(solution)/shard_map/ppermute | solution.py:21
  29.3 10.5 %copy.75 = f32[2,192,192]{0,2,1:T(8,128)} copy(f32[2,192,192]{2,1,0:T(8,128)} %slice.151) | data formatting | bytes 589824 | tf_op jit(solution)/shard_map/slice | solution.py:51
  39.8 5.3 %gather_fusion = f32[192,2]{1,0:T(8,128)} fusion(f32[2,192,192]{0,2,1:T(8,128)} %copy.75, s32[192]{0:T(256)S(1)} %bitcast.80), kind=kCustom, calls=%fused_computation | custom fusion | bytes 4608 | tf_op jit(solution)/shard_map/jit(diagonal)/gather | solution.py:62
  46.0 1.5 %convolution_add_fusion = f32[2,192,192]{2,1,0:T(8,128)S(1)} fusion(f32[2,192,192]{2,1,0:T(8,128)S(1)} %convolution_subtract_fusion.4, f32[2,64,192]{2,1,0:T(8,128)} %fusion.36, f32[8,64,192]{2,1,0:T(8,128)S(1)} %copy-done, s32[]{:T(128)S(6)} %select_n.26), kind=kOutput, calls=%fused_computation.12 | convolution fusion | flops 56696832 | bytes 917508 | tf_op jit(solution)/shard_map/bji,bjk->bik/dot_general | solution.py:33
  47.5 1.5 %fusion.14 = f32[2,192,192]{2,1,0:T(8,128)S(1)} fusion(f32[2,192,192]{2,1,0:T(8,128)S(1)} %convolution_add_fusion, f32[2,192]{1,0:T(2,128)S(1)} %copy.76, f32[192,192]{1,0:T(8,128)} %fusion.25), kind=kOutput, calls=%fused_computation.44 | convolution fusion | flops 169943040 | bytes 738816 | tf_op jit(solution)/shard_map/bij,bjk->bik/dot_general | solution.py:33
  51.8 2.1 %fusion.28 = f32[2,64,192]{2,1,0:T(8,128)} fusion(f32[2,192,192]{2,1,0:T(8,128)S(1)} %convolution_subtract_fusion.6, f32[2,64,192]{2,1,0:T(8,128)} %fusion.36, f32[2,256,256]{2,1,0:T(8,128)S(1)} %fusion.10), kind=kOutput, calls=%fused_computation.62 | convolution fusion | flops 56647680 | bytes 720896 | tf_op jit(solution)/shard_map/bij,bjk->bik/dot_general | solution.py:33
  53.9 1.8 %copy.96 = f32[2,192,64]{1,2,0:T(8,128)} copy(f32[2,192,64]{2,1,0:T(8,128)} %slice.152) | data formatting | bytes 196608
  58.1 7.4 %all_gather.12 = f32[8,64,64]{2,1,0:T(8,128)} all-gather(f32[2,64,64]{2,1,0:T(8,128)S(1)} %convolution_subtract_fusion.14), channel_id=1, replica_groups=mesh['box'=8,'nbr'=4] {'nbr'}, dimensions={0}, use_global_device_ids=true | all-gather | bytes 163840 | tf_op jit(solution)/shard_map/all_gather | solution.py:105
  65.4 10.1 %all_gather.14 = f32[8,64,192]{2,1,0:T(8,128)S(1)} all-gather(f32[2,64,192]{2,1,0:T(8,128)} %fusion.28), channel_id=1, replica_groups=mesh['box'=8,'nbr'=4] {'nbr'}, dimensions={0}, use_global_device_ids=true | all-gather | bytes 491520 | tf_op jit(solution)/shard_map/all_gather | solution.py:103
  76.1 7.5 %all_gather.15 = f32[8,192,64]{1,2,0:T(8,128)S(1)} all-gather(f32[2,192,64]{1,2,0:T(8,128)S(1)} %fusion.56), channel_id=1, replica_groups=mesh['box'=8,'nbr'=4] {'nbr'}, dimensions={0}, use_global_device_ids=true | all-gather | bytes 491520 | tf_op jit(solution)/shard_map/all_gather | solution.py:104
  83.5 2.0 %pad_maximum_fusion = f32[16,2,2,64,256]{4,3,2,1,0:T(8,128)S(1)} fusion(f32[4,2,2,64,256]{4,3,2,1,0:T(8,128)} %collective-permute-done.1, f32[8,2,2,64,256]{4,3,2,1,0:T(8,128)S(1)} %broadcast_multiply_fusion, f32[4,2,2,64,256]{4,3,2,1,0:T(8,128)} %collective-permute-done), kind=kLoop, calls=%fused_computation.1 | loop fusion | flops 2097152 | bytes 8388608 | tf_op jit(solution)/shard_map/concatenate | solution.py:22
  86.0 1.6 %fusion.2 = f32[8,2,64,256]{3,2,0,1:T(8,128)S(1)} fusion(s32[8,256]{1,0:T(8,128)S(1)} %copy-done.16, f32[16,1,2,64,256]{4,3,2,1,0:T(8,128)S(1)} %get-tuple-element.42, s32[]{:T(128)S(6)} %select_n.30), kind=kOutput, calls=%fused_computation.5 | convolution fusion | flops 805830656 | bytes 2105348 | tf_op jit(solution)/shard_map/bpik,bjk->bpij/dot_general | solution.py:33
  88.8 1.6 %fusion = f32[8,2,64,256]{3,2,1,0:T(8,128)S(1)} fusion(f32[16,1,2,64,256]{4,3,2,1,0:T(8,128)S(1)} %get-tuple-element.43, s32[]{:T(128)S(6)} %select_n.28, s32[8,256]{1,0:T(8,128)S(1)} %copy-done.16), kind=kOutput, calls=%fused_computation.3 | convolution fusion | flops 805830656 | bytes 2105348 | tf_op jit(solution)/shard_map/bpik,bjk->bpij/dot_general | solution.py:33
  95.1 2.7 %fusion.54 = f32[8,64,192]{2,1,0:T(8,128)S(1)} fusion(f32[8,64,192]{2,1,0:T(8,128)S(1)} %convolution_subtract_fusion.3, f32[8,192,192]{2,1,0:T(8,128)} %all-gather.2.cloned.1.call-done), kind=kOutput, calls=%fused_computation.90 | convolution fusion | flops 226492416 | bytes 1966080 | tf_op jit(solution)/shard_map/bij,bjk->bik/dot_general | solution.py:33
  100.4 2.2 %collective-permute-start.2 = (f32[4,64,64]{2,1,0:T(8,128)S(1)}, f32[4,64,64]{2,1,0:T(8,128)S(1)}, u32[]{:S(2)}, u32[]{:S(2)}) collective-permute-start(f32[4,64,64]{2,1,0:T(8,128)S(1)} %get-tuple-element.51), channel_id=1, source_target_pairs={{4,0},{8,4},{12,8},{16,12},{20,16},{24,20},{28,24},{0,28},{5,1},{9... | collective-permute-start | bytes 196616 | tf_op jit(solution)/shard_map/ppermute | solution.py:29
  103.4 2.8 %collective-permute-done.2 = f32[4,64,64]{2,1,0:T(8,128)S(1)} collective-permute-done((f32[4,64,64]{2,1,0:T(8,128)S(1)}, f32[4,64,64]{2,1,0:T(8,128)S(1)}, u32[]{:S(2)}, u32[]{:S(2)}) %collective-permute-start.2) | collective-permute-done | bytes 65568 | tf_op jit(solution)/shard_map/ppermute | solution.py:29
  106.2 5.3 %collective-permute-done.3 = f32[4,64,64]{2,1,0:T(8,128)S(1)} collective-permute-done((f32[4,64,64]{2,1,0:T(8,128)S(1)}, f32[4,64,64]{2,1,0:T(8,128)S(1)}, u32[]{:S(2)}, u32[]{:S(2)}) %collective-permute-start.3) | collective-permute-done | bytes 65568 | tf_op jit(solution)/shard_map/ppermute | solution.py:29
  111.8 1.4 %collective-permute-done.4 = f32[8,64,64]{2,1,0:T(8,128)S(1)} collective-permute-done((f32[8,64,64]{2,1,0:T(8,128)S(1)}, f32[8,64,64]{2,1,0:T(8,128)S(1)}, u32[]{:S(2)}, u32[]{:S(2)}) %collective-permute-start.4) | collective-permute-done | bytes 131104 | tf_op jit(solution)/shard_map/ppermute | solution.py:132
  115.6 2.3 %copy.87 = f32[8,2,64,128]{3,2,1,0:T(8,128)} copy(f32[8,2,64,128]{2,3,0,1:T(8,128)} %pad_maximum_fusion.1) | data formatting | bytes 1048576
  118.8 2.8 %collective-permute-done.5 = f32[8,64,64]{2,1,0:T(8,128)S(1)} collective-permute-done((f32[8,64,64]{2,1,0:T(8,128)S(1)}, f32[8,64,64]{2,1,0:T(8,128)S(1)}, u32[]{:S(2)}, u32[]{:S(2)}) %collective-permute-start.5) | collective-permute-done | bytes 131104 | tf_op jit(solution)/shard_map/ppermute | solution.py:132
  (89 shorter events, 29.2 us)
Async XLA Ops:
  7.2 18.5 %copy-start = (f32[8,64,192]{2,1,0:T(8,128)S(1)}, f32[8,64,192]{2,1,0:T(8,128)}, u32[]{:S(2)}) copy-start(f32[8,64,192]{2,1,0:T(8,128)} %param.11) | copy-start | bytes 1179652
  7.2 15.8 %all-to-all-start = ((f32[8,64,256]{2,1,0:T(8,128)}), f32[8,64,256]{2,1,0:T(8,128)S(1)}, u32[]{:S(2)}, u32[]{:S(2)}) async-start(f32[8,64,256]{2,1,0:T(8,128)} %param.9), calls=%async_computation | async-start | bytes 1048576 | tf_op jit(solution)/shard_map/all_to_all | solution.py:97
  11.6 83.6 %all-gather.2.cloned.1.call-start = ((), (), s32[]{:S(2)}) async-start(), calls=%async_computation.1 | async-start | bytes 1966080 | tf_op jit(solution)/shard_map/all_gather | solution.py:102
  14.2 7.6 %copy-start.16 = (s32[8,256]{1,0:T(8,128)S(1)}, s32[8,256]{1,0:T(8,128)}, u32[]{:S(2)}) copy-start(s32[8,256]{1,0:T(8,128)} %param.10) | copy-start | bytes 24580
  15.8 67.7 %collective-permute-start = (f32[4,2,2,64,256]{4,3,2,1,0:T(8,128)}, f32[4,2,2,64,256]{4,3,2,1,0:T(8,128)}, u32[]{:S(2)}, u32[]{:S(2)}) collective-permute-start(f32[4,2,2,64,256]{4,3,2,1,0:T(8,128)} %get-tuple-element.44), channel_id=1, source_target_pairs={{0,4},{4,8},{8,12},{12,16},{16,20},{20,24},{24,28},{28,0},{1,5},{5... | collective-permute-start | bytes 3145736 | tf_op jit(solution)/shard_map/ppermute | solution.py:18
  18.1 65.4 %collective-permute-start.1 = (f32[4,2,2,64,256]{4,3,2,1,0:T(8,128)}, f32[4,2,2,64,256]{4,3,2,1,0:T(8,128)}, u32[]{:S(2)}, u32[]{:S(2)}) collective-permute-start(f32[4,2,2,64,256]{4,3,2,1,0:T(8,128)} %get-tuple-element.45), channel_id=1, source_target_pairs={{4,0},{8,4},{12,8},{16,12},{20,16},{24,20},{28,24},{0,28},{5,1},{9... | collective-permute-start | bytes 3145736 | tf_op jit(solution)/shard_map/ppermute | solution.py:21
  46.0 3.0 %copy-start.15 = (f32[192,192]{1,0:T(8,128)S(1)}, f32[192,192]{1,0:T(8,128)}, u32[]{:S(2)}) copy-start(f32[192,192]{1,0:T(8,128)} %fusion.25) | copy-start | bytes 442372
  51.8 2.1 %copy-start.2 = (f32[2,192,192]{2,1,0:T(8,128)}, f32[2,192,192]{2,1,0:T(8,128)S(1)}, u32[]{:S(2)}) copy-start(f32[2,192,192]{2,1,0:T(8,128)S(1)} %convolution_subtract_fusion.6) | copy-start | bytes 884740
  53.9 21.6 %copy-start.3 = (f32[2,192,192]{2,1,0:T(8,128)S(1)}, f32[2,192,192]{2,1,0:T(8,128)}, u32[]{:S(2)}) copy-start(f32[2,192,192]{2,1,0:T(8,128)} %copy-done.2) | copy-start | bytes 884740
  88.2 3.5 %copy-start.8 = (f32[8,64,192]{2,1,0:T(8,128)}, f32[8,64,192]{2,1,0:T(8,128)S(1)}, u32[]{:S(2)}) copy-start(f32[8,64,192]{2,1,0:T(8,128)S(1)} %convolution_subtract_fusion) | copy-start | bytes 1179652
  88.8 4.9 %copy-start.4 = (f32[8,64,192]{2,1,0:T(8,128)}, f32[8,64,192]{2,1,0:T(8,128)S(1)}, u32[]{:S(2)}) copy-start(f32[8,64,192]{2,1,0:T(8,128)S(1)} %convolution_subtract_fusion.1) | copy-start | bytes 1179652
  90.5 1.9 %copy-start.10 = (f32[8,64,256]{2,1,0:T(8,128)}, f32[8,64,256]{2,1,0:T(8,128)S(1)}, u32[]{:S(2)}) copy-start(f32[8,64,256]{2,1,0:T(8,128)S(1)} %get-tuple-element.49) | copy-start | bytes 1572868
  91.1 2.6 %copy-start.6 = (f32[8,64,192]{2,1,0:T(8,128)}, f32[8,64,192]{2,1,0:T(8,128)S(1)}, u32[]{:S(2)}) copy-start(f32[8,64,192]{2,1,0:T(8,128)S(1)} %convolution_subtract_fusion.2) | copy-start | bytes 1179652
  95.1 2.7 %copy-start.7 = (f32[8,64,192]{2,1,0:T(8,128)S(1)}, f32[8,64,192]{2,1,0:T(8,128)}, u32[]{:S(2)}) copy-start(f32[8,64,192]{2,1,0:T(8,128)} %copy-done.6) | copy-start | bytes 1179652
  95.1 3.4 %copy-start.1 = (f32[8,192,192]{2,1,0:T(8,128)S(1)}, f32[8,192,192]{2,1,0:T(8,128)}, u32[]{:S(2)}) copy-start(f32[8,192,192]{2,1,0:T(8,128)} %all-gather.2.cloned.1.call-done) | copy-start | bytes 3538948
  95.1 3.4 %copy-start.5 = (f32[8,64,192]{2,1,0:T(8,128)S(1)}, f32[8,64,192]{2,1,0:T(8,128)}, u32[]{:S(2)}) copy-start(f32[8,64,192]{2,1,0:T(8,128)} %copy-done.4) | copy-start | bytes 1179652
  98.5 4.1 %copy-start.11 = (f32[8,64,256]{2,1,0:T(8,128)S(1)}, f32[8,64,256]{2,1,0:T(8,128)}, u32[]{:S(2)}) copy-start(f32[8,64,256]{2,1,0:T(8,128)} %copy-done.10) | copy-start | bytes 1572868
  100.3 11.3 %copy-start.13 = (f32[8,64,64]{1,2,0:T(8,128)S(1)}, f32[8,64,64]{1,2,0:T(8,128)}, u32[]{:S(2)}) copy-start(f32[8,64,64]{1,2,0:T(8,128)} %convolution_subtract_fusion.12) | copy-start | bytes 393220
  100.4 11.3 %copy-start.14 = (f32[8,64,64]{1,2,0:T(8,128)S(1)}, f32[8,64,64]{1,2,0:T(8,128)}, u32[]{:S(2)}) copy-start(f32[8,64,64]{1,2,0:T(8,128)} %convolution_subtract_fusion.9) | copy-start | bytes 393220
  100.4 5.8 %collective-permute-start.2 = (f32[4,64,64]{2,1,0:T(8,128)S(1)}, f32[4,64,64]{2,1,0:T(8,128)S(1)}, u32[]{:S(2)}, u32[]{:S(2)}) collective-permute-start(f32[4,64,64]{2,1,0:T(8,128)S(1)} %get-tuple-element.51), channel_id=1, source_target_pairs={{4,0},{8,4},{12,8},{16,12},{20,16},{24,20},{28,24},{0,28},{5,1},{9... | collective-permute-start | bytes 196616 | tf_op jit(solution)/shard_map/ppermute | solution.py:29
  103.3 8.2 %collective-permute-start.3 = (f32[4,64,64]{2,1,0:T(8,128)S(1)}, f32[4,64,64]{2,1,0:T(8,128)S(1)}, u32[]{:S(2)}, u32[]{:S(2)}) collective-permute-start(f32[4,64,64]{2,1,0:T(8,128)S(1)} %get-tuple-element.50), channel_id=1, source_target_pairs={{28,0},{0,4},{4,8},{8,12},{12,16},{16,20},{20,24},{24,28},{29,1},{... | collective-permute-start | bytes 196616 | tf_op jit(solution)/shard_map/ppermute | solution.py:29
  111.6 1.6 %collective-permute-start.4 = (f32[8,64,64]{2,1,0:T(8,128)S(1)}, f32[8,64,64]{2,1,0:T(8,128)S(1)}, u32[]{:S(2)}, u32[]{:S(2)}) collective-permute-start(f32[8,64,64]{2,1,0:T(8,128)S(1)} %fusion.26), channel_id=1, source_target_pairs={{0,1},{1,0},{2,3},{3,2},{4,5},{5,4},{6,7},{7,6},{8,9},{9,8},{10,11... | collective-permute-start | bytes 393224 | tf_op jit(solution)/shard_map/ppermute | solution.py:132
  113.2 8.4 %collective-permute-start.5 = (f32[8,64,64]{2,1,0:T(8,128)S(1)}, f32[8,64,64]{2,1,0:T(8,128)S(1)}, u32[]{:S(2)}, u32[]{:S(2)}) collective-permute-start(f32[8,64,64]{2,1,0:T(8,128)S(1)} %add.75), channel_id=1, source_target_pairs={{0,2},{1,3},{2,0},{3,1},{4,6},{5,7},{6,4},{7,5},{8,10},{9,11},{10,... | collective-permute-start | bytes 393224 | tf_op jit(solution)/shard_map/ppermute | solution.py:132
  114.6 7.0 %copy-start.12 = (f32[8,64,64]{2,1,0:T(8,128)S(1)}, f32[8,64,64]{2,1,0:T(8,128)}, u32[]{:S(2)}) copy-start(f32[8,64,64]{2,1,0:T(8,128)} %all_gather.12) | copy-start | bytes 393220
  (1 other events, 1.8 us)
Sparse Core Ops, SparseCore 0:
  54.0 20.9 all-gather.1
